TPU v7x, 256 devices: a whole 4x4x8 slice. The times are simulated.
256 devices in a mesh: row: 8 (over z_hi, core), col: 32 (over z_lo, y, x).
Axes of the slice: x: 4, y: 4, z: 8 (z_hi: 4, z_lo: 2; z = z_hi * 2 + z_lo), core: 2. Of those that a mesh axis runs over, the one named last changes fastest.
Arguments:
- object_in: float32 [2, 2, 2048, 8192], P(None, None, 'row', 'col'), may hold values from -4 to 4
- probe_in: float32 [2, 256, 256], replicated, may hold values from -5 to 5
- positions: int32 [8, 32, 2, 2], P('row', 'col'), may hold values from -32 to 32
- intensity: float32 [8, 32, 2, 256, 256], P('row', 'col'), may hold values from 0.1 to 8.2
Outputs:
- object_out: float32 [2, 2, 2048, 8192], P(None, None, 'row', 'col')
- probe_out: float32 [2, 256, 256], replicated
Inputs may be any that keep to these rules, and one draw needn't show every extreme that they name: positions[r, c, p] = (dy, dx) places the probe of position p on object rows r * 256 + dy to r * 256 + dy + 255 and columns c * 256 + dx to c * 256 + dx + 255.
All inputs are finite; a program needn't handle non-finite values.
Results may differ from a plain program's by a relative error of at most 0.0003.
Values sent between devices are 32-bit elements; how exact they have to be, the bound alone decides.
A program may use at most 64 MiB of HBM per device.

v0:
```python
import math
import jax
import jax.numpy as jnp
from jax import lax
from jax.sharding import Mesh
from jax.sharding import PartitionSpec as P

RIM = 32
COL = ("col_0", "col_1", "col_2")
ROW = ("row_0", "row_1")
ROW_COL = ("row_0", "row_1", "col_0", "col_1", "col_2")


def passed_along(value, axis, steps):
    count = lax.axis_size(axis)
    initial, last = (max(0, -steps), min(count, count - steps))
    return lax.ppermute(value, axis, [(source, source + steps) for source in range(initial, last)])


def extended(cells, sides, width):
    for axis, dim in sides:
        count = lax.axis_size(axis)
        ends = count - 1
        head = lax.slice_in_dim(cells, 0, width, axis=dim)
        tail = lax.slice_in_dim(cells, cells.shape[dim] - width, cells.shape[dim], axis=dim)
        cells = jnp.concatenate(
            [
                lax.ppermute(tail, axis, [(i, (i + 1) % count) for i in range(ends)]),
                cells,
                lax.ppermute(head, axis, [((i + 1) % count, i) for i in range(ends)]),
            ],
            axis=dim,
        )
    return cells


def by_axis(array, axes):
    for axis in axes:
        array = lax.psum(array, axis)
    return array


def one_axis_at_a_time(array, axes):
    for axis in axes:
        array = lax.pmax(array, axis)
    return array


def tables(extent):
    line_idx = jnp.arange(extent, dtype=jnp.int32)
    turn_count = line_idx[:, None] * line_idx[None, :] % extent
    angles = turn_count.astype(jnp.float32) * (2.0 * math.pi / extent)
    factor = 1.0 / math.sqrt(extent)
    cosine = jnp.cos(angles) * factor
    sine_tab = jnp.sin(angles) * factor
    frequency = ((line_idx + extent // 2) % extent - extent // 2).astype(jnp.float32)
    phases = (
        -math.pi * 8.0 / (extent * extent) * (frequency[:, None] ** 2 + frequency[None, :] ** 2)
    )
    return (cosine, sine_tab, jnp.cos(phases), jnp.sin(phases))


def matrices(cosine, sine_tab, orient):
    return (cosine, sine_tab, float(orient))


def transform(real_part, imag_part, tables_pair):
    cosine, sine_tab, orient = tables_pair
    high = lax.Precision.HIGHEST
    rc = jnp.einsum("byx,xk->byk", real_part, cosine, precision=high)
    rs = jnp.einsum("byx,xk->byk", real_part, sine_tab, precision=high)
    ic = jnp.einsum("byx,xk->byk", imag_part, cosine, precision=high)
    isn = jnp.einsum("byx,xk->byk", imag_part, sine_tab, precision=high)
    mid_re = rc + orient * isn
    mid_im = ic - orient * rs
    out_re = jnp.einsum("ky,byx->bkx", cosine, mid_re, precision=high) + orient * jnp.einsum(
        "ky,byx->bkx", sine_tab, mid_im, precision=high
    )
    out_im = jnp.einsum("ky,byx->bkx", cosine, mid_im, precision=high) - orient * jnp.einsum(
        "ky,byx->bkx", sine_tab, mid_re, precision=high
    )
    return (out_re, out_im)


def times_plain(first_re, first_im, second_re, second_im):
    return (
        first_re * second_re - first_im * second_im,
        first_re * second_im + first_im * second_re,
    )


def times_conj(first_re, first_im, second_re, second_im):
    return (
        first_re * second_re + first_im * second_im,
        first_re * second_im - first_im * second_re,
    )


def tile_gradient(window, probe, offsets, measured, constants):
    cosine, sine_tab, kern_re, kern_im = constants
    forward = matrices(cosine, sine_tab, 1)
    backward = matrices(cosine, sine_tab, -1)
    extent = probe.shape[-1]
    zero_idx = jnp.zeros((), jnp.int32)

    def cut_patch(offset):
        return lax.dynamic_slice(
            window, (zero_idx, zero_idx, offset[0] + RIM, offset[1] + RIM), (2, 2, extent, extent)
        )

    patches = jax.vmap(cut_patch)(offsets)
    first_re, first_im = (patches[:, 0, 0], patches[:, 0, 1])
    second_re, second_im = (patches[:, 1, 0], patches[:, 1, 1])
    probe_re, probe_im = (probe[0], probe[1])
    wave_re, wave_im = times_plain(probe_re, probe_im, first_re, first_im)
    spec_re, spec_im = transform(wave_re, wave_im, forward)
    spec_re, spec_im = times_plain(kern_re, kern_im, spec_re, spec_im)
    prop_re, prop_im = transform(spec_re, spec_im, backward)
    exit_re, exit_im = times_plain(prop_re, prop_im, second_re, second_im)
    far_re, far_im = transform(exit_re, exit_im, forward)
    excess = 2.0 * (far_re * far_re + far_im * far_im - measured)
    back_re, back_im = transform(excess * far_re, excess * far_im, backward)
    grad2_re, grad2_im = times_conj(prop_re, prop_im, back_re, back_im)
    lift_re, lift_im = times_conj(second_re, second_im, back_re, back_im)
    lift_re, lift_im = transform(lift_re, lift_im, forward)
    lift_re, lift_im = times_conj(kern_re, kern_im, lift_re, lift_im)
    enter_re, enter_im = transform(lift_re, lift_im, backward)
    grad1_re, grad1_im = times_conj(probe_re, probe_im, enter_re, enter_im)
    probe_re_g, probe_im_g = times_conj(first_re, first_im, enter_re, enter_im)
    probe_grad = jnp.stack([jnp.sum(probe_re_g, 0), jnp.sum(probe_im_g, 0)], 0)
    pieces = jnp.stack([jnp.stack([grad1_re, grad1_im], 1), jnp.stack([grad2_re, grad2_im], 1)], 1)
    gradient = jnp.zeros(window.shape, jnp.float32)
    for position in range(offsets.shape[0]):
        start_at = (zero_idx, zero_idx, offsets[position, 0] + RIM, offsets[position, 1] + RIM)
        current = lax.dynamic_slice(gradient, start_at, pieces.shape[1:])
        gradient = lax.dynamic_update_slice(gradient, current + pieces[position], start_at)
    return (gradient, probe_grad)


def turned(block):
    return jnp.swapaxes(block, 2, 3)


def cols_then_rows(gradient):
    inner_px = gradient.shape[-1] - 2 * RIM
    upper_end = RIM + inner_px
    from_right = turned(passed_along(turned(gradient[..., :RIM]), COL, -1))
    from_left = turned(passed_along(turned(gradient[..., upper_end:]), COL, 1))
    middle = gradient[..., RIM:upper_end]
    middle = middle.at[..., inner_px - RIM :].add(from_right)
    middle = middle.at[..., :RIM].add(from_left)
    from_below = passed_along(middle[:, :, :RIM, :], ROW, -1)
    from_above = passed_along(middle[:, :, upper_end:, :], ROW, 1)
    interior = middle[:, :, RIM:upper_end, :]
    interior = interior.at[:, :, inner_px - RIM :, :].add(from_below)
    interior = interior.at[:, :, :RIM, :].add(from_above)
    return interior


def local(object_in, probe_in, positions, intensity):
    extent = probe_in.shape[-1]
    constants = tables(extent)
    offsets = positions.reshape(-1, 2)
    measured = intensity.reshape(-1, extent, extent)
    tile_total = lax.axis_size(ROW) * lax.axis_size(COL)
    probe_rate = 2.0 / tile_total
    current = object_in
    window = extended(current, ((ROW, 2), (COL, 3)), RIM)
    gradient, probe_grad = tile_gradient(window, probe_in, offsets, measured, constants)
    probe_total = by_axis(probe_grad, ROW_COL)
    probe_next = probe_in - probe_rate * probe_total
    descent = cols_then_rows(gradient)
    local_peak = jnp.max(descent[:, 0] ** 2 + descent[:, 1] ** 2)
    largest = one_axis_at_a_time(local_peak, ROW_COL)
    current = current - 0.3 * descent / (jnp.sqrt(largest) + 1e-06)
    return (current, probe_next)


def solution(mesh):
    torus = Mesh(mesh.devices.reshape(4, 2, 2, 4, 4), ("row_0", "row_1", "col_0", "col_1", "col_2"))
    placed = (P(None, None, ROW, COL), P(), P(ROW, COL, None, None), P(ROW, COL, None, None, None))
    return jax.shard_map(
        local,
        mesh=torus,
        in_specs=placed,
        out_specs=(P(None, None, ROW, COL), P()),
        check_vma=False,
    )
```

profile of v0, /device:TPU:8, one launch (start us, length us, event | category | flops | bytes accessed | tf_op | source)
XLA Modules:
  0.0 397.1 jit_solution(860421095637435779)
XLA Ops:
  16.1 2.1 copy.98
  19.2 3.4 collective-permute-start.2
  22.7 4.6 %collective-permute-start.3 = (f32[2,2,320,32]{2,3,1,0:T(8,128)S(1)}, f32[2,2,320,32]{2,3,1,0:T(8,128)S(1)}, u32[]{:S(2)}, u32[]{:S(2)}) collective-permute-start(f32[2,2,320,32]{2,3,1,0:T(8,128)S(1)} %get-tuple-element.85), channel_id=1, source_target_pairs={{1,0},{2,1},{3,2},{4,3},{5,4},{6,5},{7,6},{8,7},{9,8},{10,9},{11,1... | collective-permute-start | bytes 491528 | tf_op jit(solution)/shard_map/ppermute | solution.py:30
  32.2 11.2 %while.5 = (s32[]{:T(128)}, f32[2,2,320,320]{2,3,1,0:T(8,128)S(1)}, s32[2,4]{1,0:T(2,128)S(1)}, f32[2,2,2,256,256]{3,4,0,2,1:T(8,128)}, s32[]{:T(128)}) while((s32[]{:T(128)}, f32[2,2,320,320]{2,3,1,0:T(8,128)S(1)}, s32[2,4]{1,0:T(2,128)S(1)}, f32[2,2,2,256,256]{3,4,0,2,1:T(8,128)}, s32[]{:T(128)}) %tuple.62), condition=%wide.while_cond.4, body=%wide.while_body.4.sunk | while | flops 2 | bytes 21496496 | solution.py:107
  43.4 3.4 fusion.112
  46.8 3.2 fusion.116
  57.5 2.3 fusion.22
  69.1 2.1 fusion.20
  80.4 2.1 convolution_add_fusion.3
  93.5 2.3 fusion.88
  97.8 1.9 fusion.12
  105.3 2.1 add_bitcast_fusion
  116.7 2.1 fusion.82
  128.1 2.3 fusion.4
  135.9 2.0 fusion.38
  145.6 65.6 %all-reduce.6.cloned.1.call-done = f32[2,256,256]{1,2,0:T(8,128)} async-done(((f32[2,256,256]{1,2,0:T(8,128)}), f32[2,256,256]{1,2,0:T(8,128)}) %all-reduce.6.cloned.1.call-update) | async-done | bytes 524304 | tf_op jit(solution)/shard_map/psum | solution.py:39
  211.3 2.1 fusion.25
  213.6 14.1 %dynamic_update_slice.6 = f32[2,2,320,320]{2,3,1,0:T(8,128)S(1)} dynamic-update-slice(f32[2,2,320,320]{2,3,1,0:T(8,128)S(1)} %broadcast_in_dim.2, f32[2,2,256,256]{2,3,1,0:T(8,128)} %fusion.25, s32[]{:T(128)} %constant.162.clone.1, s32[]{:T(128)} %constant.162.clone.1, s32[]{:T(128)S(6)} %select_n.155, s32[]{:T(128)S(6)} %select_n.156) | dynamic-update-slice | bytes 2097156 | tf_op jit(solution)/shard_map/dynamic_update_slice | solution.py:136
  227.7 2.4 fusion.27
  230.1 13.8 %dynamic_update_slice.7 = f32[2,2,320,320]{2,3,1,0:T(8,128)S(1)} dynamic-update-slice(f32[2,2,320,320]{2,3,1,0:T(8,128)S(1)} %dynamic_update_slice.6, f32[2,2,256,256]{2,3,1,0:T(8,128)} %fusion.27, s32[]{:T(128)} %constant.162.clone.1, s32[]{:T(128)} %constant.162.clone.1, s32[]{:T(128)S(6)} %select_n.157, s32[]{:T(128)S(6)} %select_n.158) | dynamic-update-slice | bytes 2097156 | tf_op jit(solution)/shard_map/dynamic_update_slice | solution.py:136
  244.7 4.0 %collective-permute-start.4 = (f32[2,2,32,320]{3,2,1,0:T(8,128)}, f32[2,2,32,320]{3,2,1,0:T(8,128)}, u32[]{:S(2)}, u32[]{:S(2)}) collective-permute-start(f32[2,2,32,320]{3,2,1,0:T(8,128)} %get-tuple-element.87), channel_id=1, source_target_pairs={{1,0},{2,1},{3,2},{4,3},{5,4},{6,5},{7,6},{8,7},{9,8},{10,9},{11,1... | collective-permute-start | bytes 491528 | tf_op jit(solution)/shard_map/ppermute | solution.py:17
  253.5 5.9 %collective-permute-done.5 = f32[2,2,32,320]{3,2,1,0:T(8,128)S(1)} collective-permute-done((f32[2,2,32,320]{3,2,1,0:T(8,128)S(1)}, f32[2,2,32,320]{3,2,1,0:T(8,128)S(1)}, u32[]{:S(2)}, u32[]{:S(2)}) %collective-permute-start.5) | collective-permute-done | bytes 163872 | tf_op jit(solution)/shard_map/ppermute | solution.py:17
  259.5 27.1 %all-reduce.10.cloned.1.call-done = f32[2,256,256]{1,2,0:T(8,128)} async-done(((f32[2,256,256]{1,2,0:T(8,128)}), f32[2,256,256]{1,2,0:T(8,128)}) %all-reduce.10.cloned.1.call-update) | async-done | bytes 524304 | tf_op jit(solution)/shard_map/psum | solution.py:39
  289.2 3.9 collective-permute-start.7
  293.1 2.6 scatter-add.16
  295.7 40.5 %all-reduce.12.cloned.1.call-done = f32[2,256,256]{1,2,0:T(8,128)} async-done(((f32[2,256,256]{1,2,0:T(8,128)}), f32[2,256,256]{1,2,0:T(8,128)}) %all-reduce.12.cloned.1.call-update) | async-done | bytes 524304 | tf_op jit(solution)/shard_map/psum | solution.py:39
  337.4 2.3 scatter-add.19
  340.5 13.4 %pmax.35 = f32[]{:T(128)} all-reduce(f32[]{:T(128)} %fusion.29), channel_id=1, replica_groups=mesh['row_0'=4,'row_1'=2,'col_0'=2,'col_1'=4,'col_2'=4] {'row_0'}, use_global_device_ids=true, to_apply=%region_1.2 | all-reduce | flops 1 | bytes 8 | tf_op jit(solution)/shard_map/pmax | solution.py:45
  353.8 3.1 pmax.36
  356.9 5.5 %pmax.37 = f32[]{:T(128)} all-reduce(f32[]{:T(128)} %pmax.36), channel_id=1, replica_groups=mesh['row_0'=4,'row_1'=2,'col_0'=2,'col_1'=4,'col_2'=4] {'col_0'}, use_global_device_ids=true, to_apply=%region_3.4 | all-reduce | flops 1 | bytes 8 | tf_op jit(solution)/shard_map/pmax | solution.py:45
  362.4 10.0 %pmax.38 = f32[]{:T(128)} all-reduce(f32[]{:T(128)} %pmax.37), channel_id=1, replica_groups=mesh['row_0'=4,'row_1'=2,'col_0'=2,'col_1'=4,'col_2'=4] {'col_1'}, use_global_device_ids=true, to_apply=%region_4.5 | all-reduce | flops 1 | bytes 8 | tf_op jit(solution)/shard_map/pmax | solution.py:45
  373.4 11.1 %pmax.39 = f32[]{:T(128)} all-reduce(f32[]{:T(128)} %pmax.38), channel_id=1, replica_groups=mesh['row_0'=4,'row_1'=2,'col_0'=2,'col_1'=4,'col_2'=4] {'col_2'}, use_global_device_ids=true, to_apply=%region_5.6 | all-reduce | flops 1 | bytes 8 | tf_op jit(solution)/shard_map/pmax | solution.py:45
  (139 shorter events, 113.2 us)
Async XLA Ops:
  7.2 6.2 %copy-start.11 = (f32[2,256,256]{2,1,0:T(8,128)S(1)}, f32[2,256,256]{2,1,0:T(8,128)}, u32[]{:S(2)}) copy-start(f32[2,256,256]{2,1,0:T(8,128)} %param.13) | copy-start | bytes 1572868
  7.2 204.0 %all-reduce.6.cloned.1.call-start = ((), (), s32[]{:S(2)}) async-start(), calls=%async_computation | async-start | bytes 1048576 | tf_op jit(solution)/shard_map/psum | solution.py:39
  8.8 21.6 %copy-start.2 = (f32[2,2,256,256]{2,3,1,0:T(8,128)}, f32[2,2,256,256]{2,3,1,0:T(8,128)S(1)}, u32[]{:S(2)}) copy-start(f32[2,2,256,256]{2,3,1,0:T(8,128)S(1)} %copy.124) | copy-start | bytes 3145732
  10.1 8.1 %copy-start.14 = (s32[1,1,2,2]{3,2,1,0:T(2,128)S(1)}, s32[1,1,2,2]{3,2,1,0:T(2,128)}, u32[]{:S(2)}) copy-start(s32[1,1,2,2]{3,2,1,0:T(2,128)} %param.14) | copy-start | bytes 52
  10.1 8.2 %collective-permute-start = (f32[2,2,32,256]{2,3,1,0:T(8,128)}, f32[2,2,32,256]{2,3,1,0:T(8,128)S(1)}, u32[]{:S(2)}, u32[]{:S(2)}) collective-permute-start(f32[2,2,32,256]{2,3,1,0:T(8,128)} %get-tuple-element.96), channel_id=1, source_target_pairs={{0,32},{32,64},{64,96},{96,128},{128,160},{160,192},{192,224},{1,3... | collective-permute-start | bytes 393224 | tf_op jit(solution)/shard_map/ppermute | solution.py:28
  12.0 7.0 %collective-permute-start.1 = (f32[2,2,32,256]{2,3,1,0:T(8,128)}, f32[2,2,32,256]{2,3,1,0:T(8,128)S(1)}, u32[]{:S(2)}, u32[]{:S(2)}) collective-permute-start(f32[2,2,32,256]{2,3,1,0:T(8,128)} %get-tuple-element.97), channel_id=1, source_target_pairs={{32,0},{64,32},{96,64},{128,96},{160,128},{192,160},{224,192},{33,... | collective-permute-start | bytes 393224 | tf_op jit(solution)/shard_map/ppermute | solution.py:30
  18.3 10.7 %copy-start.8 = (f32[2,2,32,256]{2,3,1,0:T(8,128)}, f32[2,2,32,256]{2,3,1,0:T(8,128)S(1)}, u32[]{:S(2)}) copy-start(f32[2,2,32,256]{2,3,1,0:T(8,128)S(1)} %collective-permute-done) | copy-start | bytes 393220
  19.0 9.9 %copy-start.9 = (f32[2,2,32,256]{2,3,1,0:T(8,128)}, f32[2,2,32,256]{2,3,1,0:T(8,128)S(1)}, u32[]{:S(2)}) copy-start(f32[2,2,32,256]{2,3,1,0:T(8,128)S(1)} %collective-permute-done.1) | copy-start | bytes 393220
  19.2 9.7 %collective-permute-start.2 = (f32[2,2,320,32]{2,3,1,0:T(8,128)S(1)}, f32[2,2,320,32]{2,3,1,0:T(8,128)S(1)}, u32[]{:S(2)}, u32[]{:S(2)}) collective-permute-start(f32[2,2,320,32]{2,3,1,0:T(8,128)S(1)} %get-tuple-element.84), channel_id=1, source_target_pairs={{0,1},{1,2},{2,3},{3,4},{4,5},{5,6},{6,7},{7,8},{8,9},{9,10},{10,1... | collective-permute-start | bytes 491528 | tf_op jit(solution)/shard_map/ppermute | solution.py:28
  22.7 7.7 %collective-permute-start.3 = (f32[2,2,320,32]{2,3,1,0:T(8,128)S(1)}, f32[2,2,320,32]{2,3,1,0:T(8,128)S(1)}, u32[]{:S(2)}, u32[]{:S(2)}) collective-permute-start(f32[2,2,320,32]{2,3,1,0:T(8,128)S(1)} %get-tuple-element.85), channel_id=1, source_target_pairs={{1,0},{2,1},{3,2},{4,3},{5,4},{6,5},{7,6},{8,7},{9,8},{10,9},{11,1... | collective-permute-start | bytes 491528 | tf_op jit(solution)/shard_map/ppermute | solution.py:30
  32.2 1.3 copy-start
  35.7 1.9 copy-start.1
  37.7 1.3 copy-start
  41.2 1.9 copy-start.1
  43.4 6.6 %copy-start.5 = (f32[256,256]{0,1:T(8,128)S(1)}, f32[256,256]{0,1:T(8,128)}, u32[]{:S(2)}) copy-start(f32[256,256]{0,1:T(8,128)} %copy.64) | copy-start | bytes 786436
  43.4 6.6 %copy-start.6 = (f32[256,256]{0,1:T(8,128)S(1)}, f32[256,256]{0,1:T(8,128)}, u32[]{:S(2)}) copy-start(f32[256,256]{0,1:T(8,128)} %copy.71) | copy-start | bytes 786436
  43.4 6.6 %copy-start.7 = (f32[2,2,2,256,256]{3,4,0,2,1:T(8,128)S(1)}, f32[2,2,2,256,256]{3,4,0,2,1:T(8,128)}, u32[]{:S(2)}) copy-start(f32[2,2,2,256,256]{3,4,0,2,1:T(8,128)} %get-tuple-element.57) | copy-start | bytes 6291460
  86.1 5.5 %copy-start.4 = (f32[1,1,2,256,256]{3,4,2,1,0:T(8,128)S(1)}, f32[1,1,2,256,256]{3,4,2,1,0:T(8,128)}, u32[]{:S(2)}) copy-start(f32[1,1,2,256,256]{3,4,2,1,0:T(8,128)} %copy.98) | copy-start | bytes 1572868
  138.8 110.0 %all-reduce.8.cloned.1.call-start = ((), (), s32[]{:S(2)}) async-start(), calls=%async_computation.1 | async-start | bytes 1048576 | tf_op jit(solution)/shard_map/psum | solution.py:39
  211.2 75.3 %all-reduce.10.cloned.1.call-start = ((), (), s32[]{:S(2)}) async-start(), calls=%async_computation.2 | async-start | bytes 1048576 | tf_op jit(solution)/shard_map/psum | solution.py:39
  244.7 7.9 %collective-permute-start.4 = (f32[2,2,32,320]{3,2,1,0:T(8,128)}, f32[2,2,32,320]{3,2,1,0:T(8,128)}, u32[]{:S(2)}, u32[]{:S(2)}) collective-permute-start(f32[2,2,32,320]{3,2,1,0:T(8,128)} %get-tuple-element.87), channel_id=1, source_target_pairs={{1,0},{2,1},{3,2},{4,3},{5,4},{6,5},{7,6},{8,7},{9,8},{10,9},{11,1... | collective-permute-start | bytes 491528 | tf_op jit(solution)/shard_map/ppermute | solution.py:17
  248.8 87.5 %all-reduce.12.cloned.1.call-start = ((), (), s32[]{:S(2)}) async-start(), calls=%async_computation.3 | async-start | bytes 1048576 | tf_op jit(solution)/shard_map/psum | solution.py:39
  248.8 0.9 copy-start.13
  249.7 9.7 %collective-permute-start.5 = (f32[2,2,32,320]{3,2,1,0:T(8,128)S(1)}, f32[2,2,32,320]{3,2,1,0:T(8,128)S(1)}, u32[]{:S(2)}, u32[]{:S(2)}) collective-permute-start(f32[2,2,32,320]{3,2,1,0:T(8,128)S(1)} %copy-done.13), channel_id=1, source_target_pairs={{0,1},{1,2},{2,3},{3,4},{4,5},{5,6},{6,7},{7,8},{8,9},{9,10},{10,1... | collective-permute-start | bytes 491528 | tf_op jit(solution)/shard_map/ppermute | solution.py:17
  286.6 101.7 %all-reduce.14.cloned.1.call-start = ((), (), s32[]{:S(2)}) async-start(), calls=%async_computation.4 | async-start | bytes 1048576 | tf_op jit(solution)/shard_map/psum | solution.py:39
  287.6 5.5 %collective-permute-start.6 = (f32[2,2,32,256]{2,3,1,0:T(8,128)S(1)}, f32[2,2,32,256]{2,3,1,0:T(8,128)S(1)}, u32[]{:S(2)}, u32[]{:S(2)}) collective-permute-start(f32[2,2,32,256]{2,3,1,0:T(8,128)S(1)} %get-tuple-element.89), channel_id=1, source_target_pairs={{32,0},{64,32},{96,64},{128,96},{160,128},{192,160},{224,192},{33,... | collective-permute-start | bytes 393224 | tf_op jit(solution)/shard_map/ppermute | solution.py:17
  289.2 47.0 %collective-permute-start.7 = (f32[2,2,32,256]{2,3,1,0:T(8,128)}, f32[2,2,32,256]{2,3,1,0:T(8,128)}, u32[]{:S(2)}, u32[]{:S(2)}) collective-permute-start(f32[2,2,32,256]{2,3,1,0:T(8,128)} %get-tuple-element.88), channel_id=1, source_target_pairs={{0,32},{32,64},{64,96},{96,128},{128,160},{160,192},{192,224},{1,3... | collective-permute-start | bytes 393224 | tf_op jit(solution)/shard_map/ppermute | solution.py:17
  336.3 36.1 %copy-start.12 = (f32[2,256,256]{2,1,0:T(8,128)S(1)}, f32[2,256,256]{2,1,0:T(8,128)}, u32[]{:S(2)}) copy-start(f32[2,256,256]{2,1,0:T(8,128)} %param.13) | copy-start | bytes 1572868
  337.4 47.8 %copy-start.3 = (f32[2,2,256,256]{2,3,1,0:T(8,128)S(1)}, f32[2,2,256,256]{2,3,1,0:T(8,128)}, u32[]{:S(2)}) copy-start(f32[2,2,256,256]{2,3,1,0:T(8,128)} %copy-done.2) | copy-start | bytes 3145732
  385.4 2.9 copy-start.10
Sparse Core Ops, SparseCore 0:
  138.9 72.2 all-reduce.5
  213.8 28.7 all-reduce.7
  248.9 37.5 all-reduce.9
  288.7 47.4 all-reduce.11
  338.4 49.8 all-reduce.13
where the time goes:
time: 402 us; the launch traced here: 397 us
  waiting for transfers between devices  146 us (36%)
  matrix products  94.1 us (23%)
  local copies, waits for them, and re-layouts  57.4 us (14%)
  blocking collectives  43 us (11%)
  starting transfers between devices  22.4 us (6%)
  between operations  20.4 us (5%)
  other arithmetic  13.9 us (3%)
    psum x5, waiting for transfers between devices, by_axis(): array = lax.psum(array, axis)  135 us
    pmax x5, blocking collectives, one_axis_at_a_time(): array = lax.pmax(array, axis)  43 us
    dynamic_update_slice x2, local copies, waits for them, and re-layouts, tile_gradient(): lax.dynamic_update_slice(gradient, current + pieces[position], start_at)  27.9 us
    dot_general x6, matrix products, transform(): ic = jnp.einsum('byx,xk->byk', imag_part, cosine, precision=high)  13.1 us
    dot_general x6, matrix products, transform(): rc = jnp.einsum('byx,xk->byk', real_part, cosine, precision=high)  12.6 us
    dot_general x6, matrix products, transform(): rs = jnp.einsum('byx,xk->byk', real_part, sine_tab, precision=high)  11.8 us
    dot_general x6, matrix products, transform(): jnp.einsum('ky,byx->bkx', sine_tab, mid_im, precision=high)  11.5 us
    dot_general x6, matrix products, transform(): isn = jnp.einsum('byx,xk->byk', imag_part, sine_tab, precision=high)  11.5 us
  transfers between devices with their start and end apart: 13, of which 9 were waited for; matrix products, arithmetic and copies ran while one was open for 13% of the time, Pallas kernels for 0%

commit v1 on v0

--- a/solution.py
+++ b/solution.py
@@ -36,7 +36,8 @@
 
 def by_axis(array, axes):
     for axis in axes:
-        array = lax.psum(array, axis)
+        z = lax.all_gather(array, axis)
+        array = jnp.sum(z, axis=0)
     return array
 
 

time: 402 us -> 428 us (1.065)
  waiting for transfers between devices: 146 us -> 156 us
  blocking collectives: 43 us -> 51.8 us
  other arithmetic: 13.9 us -> 20.1 us
    all_gather x0 -> x5, waiting for transfers between devices: none -> 143 us  [by_axis(): z = lax.all_gather(array, axis)]
    psum x5 -> x0, waiting for transfers between devices: 135 us -> none  [by_axis(): array = lax.psum(array, axis)]
    reduce_sum x0 -> x5, other arithmetic: none -> 11.3 us  [by_axis(): array = jnp.sum(z, axis=0)]
    pmax x5, blocking collectives: 43 us -> 51.8 us  [one_axis_at_a_time(): array = lax.pmax(array, axis)]
  transfers between devices with their start and end apart: 13 -> 13, of which waited for: 9 -> 9; matrix products, arithmetic and copies ran while one was open for 13% -> 11% of each run, Pallas kernels for 0% -> 0%
where the time goes in v1:
time: 428 us; the launch traced here: 421 us
  waiting for transfers between devices  156 us (36%)
  matrix products  94.7 us (22%)
  local copies, waits for them, and re-layouts  54.2 us (13%)
  blocking collectives  51.8 us (12%)
  starting transfers between devices  22.8 us (5%)
  between operations  20.5 us (5%)
  other arithmetic  20.1 us (5%)
    all_gather x5, waiting for transfers between devices, by_axis(): z = lax.all_gather(array, axis)  143 us
    pmax x5, blocking collectives, one_axis_at_a_time(): array = lax.pmax(array, axis)  51.8 us
    dynamic_update_slice x2, local copies, waits for them, and re-layouts, tile_gradient(): lax.dynamic_update_slice(gradient, current + pieces[position], start_at)  27.9 us
    dot_general x6, matrix products, transform(): ic = jnp.einsum('byx,xk->byk', imag_part, cosine, precision=high)  12.9 us
    dot_general x6, matrix products, transform(): rc = jnp.einsum('byx,xk->byk', real_part, cosine, precision=high)  12.6 us
    dot_general x6, matrix products, transform(): jnp.einsum('ky,byx->bkx', sine_tab, mid_im, precision=high)  12.4 us
    dot_general x6, matrix products, transform(): isn = jnp.einsum('byx,xk->byk', imag_part, sine_tab, precision=high)  11.7 us
    dot_general x6, matrix products, transform(): rs = jnp.einsum('byx,xk->byk', real_part, sine_tab, precision=high)  11.7 us
  transfers between devices with their start and end apart: 13, of which 9 were waited for; matrix products, arithmetic and copies ran while one was open for 11% of the time, Pallas kernels for 0%

profile of v1, /device:TPU:8, one launch (start us, length us, event | category | flops | bytes accessed | tf_op | source)
XLA Modules:
  0.0 420.8 jit_solution(17112469551110878832)
XLA Ops:
  19.2 3.4 collective-permute-start.2
  22.6 4.6 %collective-permute-start.3 = (f32[2,2,320,32]{2,3,1,0:T(8,128)S(1)}, f32[2,2,320,32]{2,3,1,0:T(8,128)S(1)}, u32[]{:S(2)}, u32[]{:S(2)}) collective-permute-start(f32[2,2,320,32]{2,3,1,0:T(8,128)S(1)} %get-tuple-element.85), channel_id=1, source_target_pairs={{1,0},{2,1},{3,2},{4,3},{5,4},{6,5},{7,6},{8,7},{9,8},{10,9},{11,1... | collective-permute-start | bytes 491528 | tf_op jit(solution)/shard_map/ppermute | solution.py:30
  32.2 11.6 %while.5 = (s32[]{:T(128)}, f32[2,2,320,320]{2,3,1,0:T(8,128)S(1)}, s32[2,4]{1,0:T(2,128)S(1)}, f32[2,2,2,256,256]{3,4,0,2,1:T(8,128)}, s32[]{:T(128)}) while((s32[]{:T(128)}, f32[2,2,320,320]{2,3,1,0:T(8,128)S(1)}, s32[2,4]{1,0:T(2,128)S(1)}, f32[2,2,2,256,256]{3,4,0,2,1:T(8,128)}, s32[]{:T(128)}) %tuple.63), condition=%wide.while_cond.4, body=%wide.while_body.4.sunk | while | flops 2 | bytes 21496496 | solution.py:108
  43.8 3.4 fusion.112
  47.2 3.2 fusion.116
  80.5 2.3 convolution_add_fusion.3
  93.9 2.1 fusion.88
  105.4 2.2 add_bitcast_fusion
  116.8 2.3 fusion.82
  136.0 2.9 fusion.38
  140.0 69.2 %all-gather.11.cloned.1.call-done = f32[8,256,256]{2,1,0:T(8,128)} async-done(((f32[2,256,256]{2,1,0:T(8,128)}), f32[8,256,256]{2,1,0:T(8,128)}) %all-gather.11.cloned.1.call-update) | async-done | bytes 2097168 | tf_op jit(solution)/shard_map/all_gather | solution.py:39
  209.2 2.6 reduce_sum.65
  211.9 13.5 %all-gather.13.cloned.1.call-done = f32[4,256,256]{2,1,0:T(8,128)} async-done(((f32[2,256,256]{2,1,0:T(8,128)}), f32[4,256,256]{2,1,0:T(8,128)}) %all-gather.13.cloned.1.call-update) | async-done | bytes 1048592 | tf_op jit(solution)/shard_map/all_gather | solution.py:39
  225.4 2.2 reduce_sum.66
  227.7 27.8 %all-gather.15.cloned.1.call-done = f32[4,256,256]{2,1,0:T(8,128)} async-done(((f32[2,256,256]{2,1,0:T(8,128)}), f32[4,256,256]{2,1,0:T(8,128)}) %all-gather.15.cloned.1.call-update) | async-done | bytes 1048592 | tf_op jit(solution)/shard_map/all_gather | solution.py:39
  255.5 2.1 reduce_sum.67
  257.7 32.9 %all-gather.17.cloned.1.call-done = f32[8,256,256]{2,1,0:T(8,128)} async-done(((f32[2,256,256]{2,1,0:T(8,128)}), f32[8,256,256]{2,1,0:T(8,128)}) %all-gather.17.cloned.1.call-update) | async-done | bytes 2097168 | tf_op jit(solution)/shard_map/all_gather | solution.py:39
  290.6 2.6 reduce_sum.68
  300.4 14.1 %dynamic_update_slice.6 = f32[2,2,320,320]{2,3,1,0:T(8,128)S(1)} dynamic-update-slice(f32[2,2,320,320]{2,3,1,0:T(8,128)S(1)} %broadcast_in_dim.2, f32[2,2,256,256]{2,3,1,0:T(8,128)} %fusion.25, s32[]{:T(128)} %constant.162.clone.1, s32[]{:T(128)} %constant.162.clone.1, s32[]{:T(128)S(6)} %select_n.155, s32[]{:T(128)S(6)} %select_n.156) | dynamic-update-slice | bytes 2097156 | tf_op jit(solution)/shard_map/dynamic_update_slice | solution.py:137
  314.6 2.4 fusion.27
  317.0 13.8 %dynamic_update_slice.7 = f32[2,2,320,320]{2,3,1,0:T(8,128)S(1)} dynamic-update-slice(f32[2,2,320,320]{2,3,1,0:T(8,128)S(1)} %dynamic_update_slice.6, f32[2,2,256,256]{2,3,1,0:T(8,128)} %fusion.27, s32[]{:T(128)} %constant.162.clone.1, s32[]{:T(128)} %constant.162.clone.1, s32[]{:T(128)S(6)} %select_n.157, s32[]{:T(128)S(6)} %select_n.158) | dynamic-update-slice | bytes 2097156 | tf_op jit(solution)/shard_map/dynamic_update_slice | solution.py:137
  330.8 5.0 %collective-permute-start.4 = (f32[2,2,32,320]{3,2,1,0:T(8,128)S(1)}, f32[2,2,32,320]{3,2,1,0:T(8,128)S(1)}, u32[]{:S(2)}, u32[]{:S(2)}) collective-permute-start(f32[2,2,32,320]{3,2,1,0:T(8,128)S(1)} %get-tuple-element.87), channel_id=1, source_target_pairs={{1,0},{2,1},{3,2},{4,3},{5,4},{6,5},{7,6},{8,7},{9,8},{10,9},{11,1... | collective-permute-start | bytes 491528 | tf_op jit(solution)/shard_map/ppermute | solution.py:17
  337.9 2.4 collective-permute-done.4
  340.3 6.3 %collective-permute-done.5 = f32[2,2,32,320]{3,2,1,0:T(8,128)S(1)} collective-permute-done((f32[2,2,32,320]{3,2,1,0:T(8,128)S(1)}, f32[2,2,32,320]{3,2,1,0:T(8,128)S(1)}, u32[]{:S(2)}, u32[]{:S(2)}) %collective-permute-start.5) | collective-permute-done | bytes 163872 | tf_op jit(solution)/shard_map/ppermute | solution.py:17
  348.5 3.3 collective-permute-start.7
  351.9 2.4 scatter-add.16
  354.3 2.3 scatter-add.19
  357.4 26.3 %pmax.35 = f32[]{:T(128)} all-reduce(f32[]{:T(128)} %fusion.29), channel_id=1, replica_groups=mesh['row_0'=4,'row_1'=2,'col_0'=2,'col_1'=4,'col_2'=4] {'row_0'}, use_global_device_ids=true, to_apply=%region_1.2 | all-reduce | flops 1 | bytes 8 | tf_op jit(solution)/shard_map/pmax | solution.py:46
  383.7 3.1 pmax.36
  386.8 5.5 %pmax.37 = f32[]{:T(128)} all-reduce(f32[]{:T(128)} %pmax.36), channel_id=1, replica_groups=mesh['row_0'=4,'row_1'=2,'col_0'=2,'col_1'=4,'col_2'=4] {'col_0'}, use_global_device_ids=true, to_apply=%region_3.4 | all-reduce | flops 1 | bytes 8 | tf_op jit(solution)/shard_map/pmax | solution.py:46
  392.3 8.5 %pmax.38 = f32[]{:T(128)} all-reduce(f32[]{:T(128)} %pmax.37), channel_id=1, replica_groups=mesh['row_0'=4,'row_1'=2,'col_0'=2,'col_1'=4,'col_2'=4] {'col_1'}, use_global_device_ids=true, to_apply=%region_4.5 | all-reduce | flops 1 | bytes 8 | tf_op jit(solution)/shard_map/pmax | solution.py:46
  400.8 8.3 %pmax.39 = f32[]{:T(128)} all-reduce(f32[]{:T(128)} %pmax.38), channel_id=1, replica_groups=mesh['row_0'=4,'row_1'=2,'col_0'=2,'col_1'=4,'col_2'=4] {'col_2'}, use_global_device_ids=true, to_apply=%region_5.6 | all-reduce | flops 1 | bytes 8 | tf_op jit(solution)/shard_map/pmax | solution.py:46
  (142 shorter events, 116.7 us)
Async XLA Ops:
  7.2 6.2 %copy-start.11 = (f32[2,256,256]{2,1,0:T(8,128)S(1)}, f32[2,256,256]{2,1,0:T(8,128)}, u32[]{:S(2)}) copy-start(f32[2,256,256]{2,1,0:T(8,128)} %param.13) | copy-start | bytes 1572868
  7.2 202.0 %all-gather.11.cloned.1.call-start = ((), (), s32[]{:S(2)}) async-start(), calls=%async_computation | async-start | bytes 2621440 | tf_op jit(solution)/shard_map/all_gather | solution.py:39
  8.8 21.5 %copy-start.2 = (f32[2,2,256,256]{2,3,1,0:T(8,128)}, f32[2,2,256,256]{2,3,1,0:T(8,128)S(1)}, u32[]{:S(2)}) copy-start(f32[2,2,256,256]{2,3,1,0:T(8,128)S(1)} %copy.124) | copy-start | bytes 3145732
  10.1 8.1 %copy-start.14 = (s32[1,1,2,2]{3,2,1,0:T(2,128)S(1)}, s32[1,1,2,2]{3,2,1,0:T(2,128)}, u32[]{:S(2)}) copy-start(s32[1,1,2,2]{3,2,1,0:T(2,128)} %param.14) | copy-start | bytes 52
  10.1 8.1 %collective-permute-start = (f32[2,2,32,256]{2,3,1,0:T(8,128)}, f32[2,2,32,256]{2,3,1,0:T(8,128)S(1)}, u32[]{:S(2)}, u32[]{:S(2)}) collective-permute-start(f32[2,2,32,256]{2,3,1,0:T(8,128)} %get-tuple-element.96), channel_id=1, source_target_pairs={{0,32},{32,64},{64,96},{96,128},{128,160},{160,192},{192,224},{1,3... | collective-permute-start | bytes 393224 | tf_op jit(solution)/shard_map/ppermute | solution.py:28
  12.0 7.0 %collective-permute-start.1 = (f32[2,2,32,256]{2,3,1,0:T(8,128)}, f32[2,2,32,256]{2,3,1,0:T(8,128)S(1)}, u32[]{:S(2)}, u32[]{:S(2)}) collective-permute-start(f32[2,2,32,256]{2,3,1,0:T(8,128)} %get-tuple-element.97), channel_id=1, source_target_pairs={{32,0},{64,32},{96,64},{128,96},{160,128},{192,160},{224,192},{33,... | collective-permute-start | bytes 393224 | tf_op jit(solution)/shard_map/ppermute | solution.py:30
  18.2 10.7 %copy-start.9 = (f32[2,2,32,256]{2,3,1,0:T(8,128)}, f32[2,2,32,256]{2,3,1,0:T(8,128)S(1)}, u32[]{:S(2)}) copy-start(f32[2,2,32,256]{2,3,1,0:T(8,128)S(1)} %collective-permute-done) | copy-start | bytes 393220
  19.0 9.9 %copy-start.10 = (f32[2,2,32,256]{2,3,1,0:T(8,128)}, f32[2,2,32,256]{2,3,1,0:T(8,128)S(1)}, u32[]{:S(2)}) copy-start(f32[2,2,32,256]{2,3,1,0:T(8,128)S(1)} %collective-permute-done.1) | copy-start | bytes 393220
  19.2 9.7 %collective-permute-start.2 = (f32[2,2,320,32]{2,3,1,0:T(8,128)S(1)}, f32[2,2,320,32]{2,3,1,0:T(8,128)S(1)}, u32[]{:S(2)}, u32[]{:S(2)}) collective-permute-start(f32[2,2,320,32]{2,3,1,0:T(8,128)S(1)} %get-tuple-element.84), channel_id=1, source_target_pairs={{0,1},{1,2},{2,3},{3,4},{4,5},{5,6},{6,7},{7,8},{8,9},{9,10},{10,1... | collective-permute-start | bytes 491528 | tf_op jit(solution)/shard_map/ppermute | solution.py:28
  22.6 7.7 %collective-permute-start.3 = (f32[2,2,320,32]{2,3,1,0:T(8,128)S(1)}, f32[2,2,320,32]{2,3,1,0:T(8,128)S(1)}, u32[]{:S(2)}, u32[]{:S(2)}) collective-permute-start(f32[2,2,320,32]{2,3,1,0:T(8,128)S(1)} %get-tuple-element.85), channel_id=1, source_target_pairs={{1,0},{2,1},{3,2},{4,3},{5,4},{6,5},{7,6},{8,7},{9,8},{10,9},{11,1... | collective-permute-start | bytes 491528 | tf_op jit(solution)/shard_map/ppermute | solution.py:30
  32.2 1.3 copy-start
  35.8 1.9 copy-start.1
  37.8 1.3 copy-start
  41.4 1.9 copy-start.1
  43.8 6.6 %copy-start.6 = (f32[256,256]{0,1:T(8,128)S(1)}, f32[256,256]{0,1:T(8,128)}, u32[]{:S(2)}) copy-start(f32[256,256]{0,1:T(8,128)} %copy.64) | copy-start | bytes 786436
  43.8 6.6 %copy-start.7 = (f32[256,256]{0,1:T(8,128)S(1)}, f32[256,256]{0,1:T(8,128)}, u32[]{:S(2)}) copy-start(f32[256,256]{0,1:T(8,128)} %copy.71) | copy-start | bytes 786436
  43.8 6.6 %copy-start.8 = (f32[2,2,2,256,256]{3,4,0,2,1:T(8,128)S(1)}, f32[2,2,2,256,256]{3,4,0,2,1:T(8,128)}, u32[]{:S(2)}) copy-start(f32[2,2,2,256,256]{3,4,0,2,1:T(8,128)} %get-tuple-element.57) | copy-start | bytes 6291460
  86.4 5.5 %copy-start.4 = (f32[1,1,2,256,256]{3,4,2,1,0:T(8,128)S(1)}, f32[1,1,2,256,256]{3,4,2,1,0:T(8,128)}, u32[]{:S(2)}) copy-start(f32[1,1,2,256,256]{3,4,2,1,0:T(8,128)} %copy.98) | copy-start | bytes 1572868
  140.0 85.4 %all-gather.13.cloned.1.call-start = ((), (), s32[]{:S(2)}) async-start(), calls=%async_computation.1 | async-start | bytes 1572864 | tf_op jit(solution)/shard_map/all_gather | solution.py:39
  211.8 43.7 %all-gather.15.cloned.1.call-start = ((), (), s32[]{:S(2)}) async-start(), calls=%async_computation.2 | async-start | bytes 1572864 | tf_op jit(solution)/shard_map/all_gather | solution.py:39
  227.6 63.0 %all-gather.17.cloned.1.call-start = ((), (), s32[]{:S(2)}) async-start(), calls=%async_computation.3 | async-start | bytes 2621440 | tf_op jit(solution)/shard_map/all_gather | solution.py:39
  257.6 41.2 %copy-start.13 = (f32[2,1,256,256]{2,3,0,1:T(8,128)S(1)}, f32[2,1,256,256]{2,3,0,1:T(8,128)}, u32[]{:S(2)}) copy-start(f32[2,1,256,256]{2,3,0,1:T(8,128)} %get-tuple-element.93) | copy-start | bytes 1572868
  257.7 153.7 %all-gather.19.cloned.1.call-start = ((), (), s32[]{:S(2)}) async-start(), calls=%async_computation.4 | async-start | bytes 2621440 | tf_op jit(solution)/shard_map/all_gather | solution.py:39
  299.0 1.3 copy-start.5
  330.8 9.4 %collective-permute-start.4 = (f32[2,2,32,320]{3,2,1,0:T(8,128)S(1)}, f32[2,2,32,320]{3,2,1,0:T(8,128)S(1)}, u32[]{:S(2)}, u32[]{:S(2)}) collective-permute-start(f32[2,2,32,320]{3,2,1,0:T(8,128)S(1)} %get-tuple-element.87), channel_id=1, source_target_pairs={{1,0},{2,1},{3,2},{4,3},{5,4},{6,5},{7,6},{8,7},{9,8},{10,9},{11,1... | collective-permute-start | bytes 491528 | tf_op jit(solution)/shard_map/ppermute | solution.py:17
  335.9 10.7 %collective-permute-start.5 = (f32[2,2,32,320]{3,2,1,0:T(8,128)S(1)}, f32[2,2,32,320]{3,2,1,0:T(8,128)S(1)}, u32[]{:S(2)}, u32[]{:S(2)}) collective-permute-start(f32[2,2,32,320]{3,2,1,0:T(8,128)S(1)} %get-tuple-element.86), channel_id=1, source_target_pairs={{0,1},{1,2},{2,3},{3,4},{4,5},{5,6},{6,7},{7,8},{8,9},{9,10},{10,1... | collective-permute-start | bytes 491528 | tf_op jit(solution)/shard_map/ppermute | solution.py:17
  346.9 4.9 %collective-permute-start.6 = (f32[2,2,32,256]{2,3,1,0:T(8,128)S(1)}, f32[2,2,32,256]{2,3,1,0:T(8,128)S(1)}, u32[]{:S(2)}, u32[]{:S(2)}) collective-permute-start(f32[2,2,32,256]{2,3,1,0:T(8,128)S(1)} %get-tuple-element.89), channel_id=1, source_target_pairs={{32,0},{64,32},{96,64},{128,96},{160,128},{192,160},{224,192},{33,... | collective-permute-start | bytes 393224 | tf_op jit(solution)/shard_map/ppermute | solution.py:17
  348.5 5.8 %collective-permute-start.7 = (f32[2,2,32,256]{2,3,1,0:T(8,128)S(1)}, f32[2,2,32,256]{2,3,1,0:T(8,128)S(1)}, u32[]{:S(2)}, u32[]{:S(2)}) collective-permute-start(f32[2,2,32,256]{2,3,1,0:T(8,128)S(1)} %get-tuple-element.88), channel_id=1, source_target_pairs={{0,32},{32,64},{64,96},{96,128},{128,160},{160,192},{192,224},{1,3... | collective-permute-start | bytes 393224 | tf_op jit(solution)/shard_map/ppermute | solution.py:17
  354.3 55.6 %copy-start.3 = (f32[2,2,256,256]{2,3,1,0:T(8,128)S(1)}, f32[2,2,256,256]{2,3,1,0:T(8,128)}, u32[]{:S(2)}) copy-start(f32[2,2,256,256]{2,3,1,0:T(8,128)} %copy-done.2) | copy-start | bytes 3145732
  410.0 3.1 copy-start.12
Sparse Core Ops, SparseCore 0:
  140.1 69.0 all-gather.10
  211.9 13.4 all-gather.12
  227.7 27.7 all-gather.14
  257.8 32.7 all-gather.16
  293.3 34.2 all-gather.18
